TPU v7x, 32 devices: a whole 2x2x4 slice. The times are simulated.
32 devices in a mesh: face: 4 (over z), strip: 8 (over y, x, core).
Axes of the slice: x: 2, y: 2, z: 4, core: 2. Of those that a mesh axis runs over, the one named last changes fastest.
Arguments:
- pixels_in: bfloat16 [4, 8, 64, 1024], P('face', 'strip'), may hold values from -6 to 6
- w_qkv: bfloat16 [1024, 3072], P(None, 'face'), may hold values from -0.1875 to 0.1875
- w_gate: bfloat16 [1024, 32], P(None, 'face'), may hold values from -0.1875 to 0.1875
- decay_rate: float32 [16], replicated, may hold values from 0.0005859375 to 0.05
- beta_bias: float32 [16], replicated, may hold values from -4 to 1
Outputs:
- mixed: bfloat16 [4, 8, 64, 1024], P('face', 'strip')
All inputs are finite; a program needn't handle non-finite values.
Results may differ from a plain program's by a relative error of at most 0.0069.
Values may be sent and summed in bfloat16 or wider, within the bound.
A program may use at most 192 MiB of HBM per device.

v0:
```python
import jax
import jax.numpy as jnp
from jax import lax
from jax.sharding import PartitionSpec as P

highest = lax.Precision.HIGHEST


def carried_in(part, axis, combine, identity):
    place = lax.axis_index(axis)
    gathered = jax.tree.map(lambda a: lax.all_gather(a, axis), part)
    state = jax.tree.map(lambda a, e: jnp.zeros_like(a) + jnp.asarray(e, a.dtype), part, identity)

    def one(turn, state):
        return combine(
            state, jax.tree.map(lambda a: lax.dynamic_index_in_dim(a, turn, 0, False), gathered)
        )

    return lax.fori_loop(0, place, one, state)


def unit_rows(tensor):
    return tensor / jnp.sqrt(jnp.sum(tensor * tensor, axis=-1, keepdims=True) + 1e-06)


def head_norm(tensor):
    normed = tensor / jnp.sqrt(jnp.mean(tensor * tensor, axis=-1, keepdims=True) + 1e-06)
    return normed.reshape(tensor.shape[0], -1)


def project(flat_px, w_full, gate_full):
    projected = jnp.dot(flat_px, w_full, preferred_element_type=jnp.float32).astype(jnp.bfloat16)
    gate_logits = jnp.dot(flat_px, gate_full, preferred_element_type=jnp.float32).astype(
        jnp.bfloat16
    )
    return (projected, gate_logits)


def unpack(projected, gate_logits, decay_rate, beta_bias):
    heads = decay_rate.shape[0]
    count = projected.shape[0]
    parts = projected.astype(jnp.float32).reshape(count, 3, heads, -1)
    logits = gate_logits.astype(jnp.float32)
    log_decay = -decay_rate[None, :] * jnp.exp(logits[:, :heads])
    strength = jax.nn.sigmoid(logits[:, heads:] + beta_bias[None, :])
    return (unit_rows(parts[:, 0]), unit_rows(parts[:, 1]), parts[:, 2], log_decay, strength)


def group_terms(queries, key_rows, val_rows, log_decay, strength):
    span = queries.shape[1]
    width = queries.shape[2]
    cumulative = jnp.cumsum(log_decay, axis=1)
    gap_log = cumulative[:, :, None] - cumulative[:, None, :]
    row_ids = lax.broadcasted_iota(jnp.int32, (span, span), 0)
    col_ids = lax.broadcasted_iota(jnp.int32, (span, span), 1)
    inclusive = row_ids >= col_ids
    strict = row_ids > col_ids
    within = jnp.where(inclusive, jnp.exp(jnp.where(inclusive, gap_log, 0.0)), 0.0)
    key_dot = jnp.einsum("hck,hjk->hcj", key_rows, key_rows, precision=highest)
    lower_part = jnp.where(strict, within * key_dot, 0.0) * strength[:, :, None]
    system = lower_part + jnp.eye(span, dtype=queries.dtype)
    scale_all = jnp.exp(cumulative)
    rhs_values = val_rows * strength[:, :, None]
    rhs_keys = key_rows * (strength * scale_all)[:, :, None]
    solved = lax.linalg.triangular_solve(
        system,
        jnp.concatenate([rhs_values, rhs_keys], axis=-1),
        left_side=True,
        lower=True,
        unit_diagonal=True,
    )
    new_values = solved[..., :width]
    mixing = solved[..., width:]
    scores = jnp.where(
        inclusive, within * jnp.einsum("hck,hjk->hcj", queries, key_rows, precision=highest), 0.0
    )
    tail_decay = jnp.exp(cumulative[:, -1:] - cumulative)
    weighted_keys = key_rows * tail_decay[:, :, None]
    end_scale = jnp.exp(cumulative[:, -1])
    transition = end_scale[:, None, None] * jnp.eye(width, dtype=queries.dtype) - jnp.einsum(
        "hck,hcj->hkj", mixing, weighted_keys, precision=highest
    )
    writes = jnp.einsum("hcv,hck->hvk", new_values, weighted_keys, precision=highest)
    effective_query = queries * scale_all[:, :, None] - jnp.einsum(
        "hcj,hjk->hck", scores, mixing, precision=highest
    )
    local_out = jnp.einsum("hcj,hjv->hcv", scores, new_values, precision=highest)
    return (local_out, effective_query, transition, writes)


def to_blocks(queries, key_rows, val_rows, log_decay, strength):
    count = queries.shape[0] // 64

    def shape_four(tensor):
        return tensor.reshape(count, 64, tensor.shape[1], tensor.shape[2]).transpose(0, 2, 1, 3)

    def shape_three(tensor):
        return tensor.reshape(count, 64, tensor.shape[1]).transpose(0, 2, 1)

    return (
        shape_four(queries),
        shape_four(key_rows),
        shape_four(val_rows),
        shape_three(log_decay),
        shape_three(strength),
    )


def from_blocks(outputs):
    count, heads, span, width = outputs.shape
    return outputs.transpose(0, 2, 1, 3).reshape(count * span, heads, width)


def carried(prefix, local_state, eye_block, zero_state):

    def compose(earlier, later):
        joined_map = jnp.einsum("hkj,hjl->hkl", earlier[0], later[0], precision=highest)
        joined_state = (
            jnp.einsum("hvk,hkj->hvj", earlier[1], later[0], precision=highest) + later[1]
        )
        return (joined_map, joined_state)

    _, incoming = carried_in((prefix, local_state), "strip", compose, (eye_block, zero_state))
    return incoming


def strip_scan(queries, key_rows, val_rows, log_decay, strength):
    blocks = to_blocks(queries, key_rows, val_rows, log_decay, strength)
    heads = queries.shape[1]
    width = queries.shape[2]
    eye_block = jnp.broadcast_to(jnp.eye(width, dtype=jnp.float32), (heads, width, width))
    zero_state = jnp.zeros((heads, width, width), jnp.float32)

    def advance_local(carry, block_in):
        carry_state, prefix = carry
        local_out, effective_query, transition, writes = group_terms(*block_in)
        outputs = local_out + jnp.einsum(
            "hck,hvk->hcv", effective_query, carry_state, precision=highest
        )
        lifted = jnp.einsum("hck,hjk->hcj", effective_query, prefix, precision=highest)
        carry_state = (
            jnp.einsum("hvk,hkj->hvj", carry_state, transition, precision=highest) + writes
        )
        prefix = jnp.einsum("hkj,hjl->hkl", prefix, transition, precision=highest)
        return ((carry_state, prefix), (outputs, lifted))

    (local_state, prefix), (outputs, lifted) = lax.scan(
        advance_local, (zero_state, eye_block), blocks
    )
    incoming = carried(prefix, local_state, eye_block, zero_state)
    outputs = outputs + jnp.einsum("nhcj,hvj->nhcv", lifted, incoming, precision=highest)
    return from_blocks(outputs)


def on_device(pixels_in, w_qkv, w_gate, decay_rate, beta_bias):
    w_full, gate_full = (
        lax.all_gather(w_qkv, "face", axis=1, tiled=True),
        lax.all_gather(w_gate, "face", axis=1, tiled=True),
    )
    rows_here = pixels_in.shape[1]
    width_cols = pixels_in.shape[2]
    features = pixels_in.shape[3]
    n_strip = lax.axis_size("strip")
    cols_here = width_cols // n_strip
    tall_rows = rows_here * n_strip
    plane = pixels_in.reshape(rows_here, width_cols, features)
    projected, gate_logits = project(
        plane.reshape(rows_here * width_cols, features), w_full, gate_full
    )
    row_out = strip_scan(*unpack(projected, gate_logits, decay_rate, beta_bias))
    arrived_proj, arrived_gates = (
        lax.all_to_all(
            projected.reshape(rows_here, width_cols, -1),
            "strip",
            split_axis=1,
            concat_axis=0,
            tiled=True,
        ),
        lax.all_to_all(
            gate_logits.reshape(rows_here, width_cols, -1),
            "strip",
            split_axis=1,
            concat_axis=0,
            tiled=True,
        ),
    )
    col_proj = arrived_proj.swapaxes(0, 1).reshape(tall_rows * cols_here, -1)
    col_gates = arrived_gates.swapaxes(0, 1).reshape(tall_rows * cols_here, -1)
    col_out = strip_scan(*unpack(col_proj, col_gates, decay_rate, beta_bias))
    col_mixed = head_norm(col_out).astype(jnp.bfloat16)
    col_tall = col_mixed.reshape(cols_here, tall_rows, -1).swapaxes(0, 1)
    returned = lax.all_to_all(col_tall, "strip", split_axis=0, concat_axis=1, tiled=True)
    row_mixed = head_norm(row_out).reshape(rows_here, width_cols, -1)
    mixed = (row_mixed + returned.astype(jnp.float32)).astype(jnp.bfloat16)
    return mixed[None]


def solution(mesh):
    in_specs = (P("face", "strip", None, None), P(None, "face"), P(None, "face"), P(), P())
    out_specs = P("face", "strip", None, None)
    return jax.shard_map(
        on_device, mesh=mesh, in_specs=in_specs, out_specs=out_specs, check_vma=False
    )
```

profile of v0, /device:TPU:0, one launch (start us, length us, event | category | flops | bytes accessed | tf_op | source)
XLA Modules:
  0.0 444.7 jit_solution(4246070837941400303)
XLA Ops:
  6.5 0.7 all-gather.10.cloned.1.call-update
  7.3 15.1 %all_gather.30 = bf16[1024,32]{0,1:T(8,128)(2,1)S(1)} all-gather(bf16[1024,8]{0,1:T(8,128)(2,1)} %param.13), channel_id=1, replica_groups=mesh['face'=4,'strip'=8] {'face'}, dimensions={1}, use_global_device_ids=true | all-gather | bytes 81920 | tf_op jit(solution)/shard_map/all_gather | solution.py:158
  22.7 0.6 broadcast.170
  23.3 0.8 reduce.10
  24.1 0.7 reshape.328
  24.7 3.7 all-to-all-start
  28.7 0.7 neg.11
  29.4 3.8 all-to-all-done
  34.4 1.4 exponential_multiply_fusion.1
  35.7 91.3 %all-gather.10.cloned.1.call-done = bf16[1024,3072]{1,0:T(8,128)(2,1)} async-done(((bf16[1024,768]{1,0:T(8,128)(2,1)}), bf16[1024,3072]{1,0:T(8,128)(2,1)}) %all-gather.10.cloned.1.call-update) | async-done | bytes 6291472 | tf_op jit(solution)/shard_map/all_gather | solution.py:157
  127.0 4.0 convolution_convert_fusion
  131.0 0.4 reshape.312
  131.4 1.0 fusion.95
  132.7 1.4 fusion.19
  134.1 78.6 %custom-call.4 = f32[16,1,64,64]{2,3,1,0:T(8,128)S(1)} custom-call(f32[16,1,64,64]{3,2,1,0:T(8,128)S(1)} %fusion.19), custom_call_target="InvertDiagBlocksLowerTriangular" | custom-call | tf_op jit(solution)/shard_map/while/body/eval_jaxpr/triangular_solve/custom-call.1 | solution.py:65
  212.7 0.5 fusion.36
  213.2 1.1 fusion.27
  214.4 1.4 convolution_subtract_fusion.2
  215.8 1.4 fusion.67
  217.2 0.6 all-gather.14.cloned.1.call-start
  217.8 0.6 fusion.70
  218.4 2.1 convolution_add_fusion.2
  220.5 0.6 copy.228
  221.1 3.0 reduce.11
  224.2 1.0 reshape.330
  225.2 3.6 all-to-all-start.1
  229.0 0.6 exp.84
  229.6 7.5 %all-to-all-done.1 = bf16[8,2,12288]{2,1,0:T(2,128)(2,1)S(1)} async-done(((bf16[8,2,12288]{2,1,0:T(2,128)(2,1)}), bf16[8,2,12288]{2,1,0:T(2,128)(2,1)S(1)}, u32[]{:S(2)}, u32[]{:S(2)}) %all-to-all-start.1) | async-done | bytes 393248 | tf_op jit(solution)/shard_map/all_to_all | solution.py:172
  237.1 0.4 reshape.331
  237.5 0.8 bitcast_convert_fusion
  238.5 0.5 copy.226
  238.9 0.4 reshape.314
  239.4 1.1 fusion.94
  240.5 0.2 multiply_reduce_fusion.1
  240.8 2.2 fusion.23
  243.0 79.3 %custom-call.5 = f32[16,1,64,64]{2,3,1,0:T(8,128)} custom-call(f32[16,1,64,64]{3,2,1,0:T(8,128)S(1)} %fusion.23), custom_call_target="InvertDiagBlocksLowerTriangular" | custom-call | tf_op jit(solution)/shard_map/while/body/eval_jaxpr/triangular_solve/custom-call.1 | solution.py:65
  322.3 0.5 fusion.35
  322.8 2.2 fusion.31
  325.0 1.4 convolution_subtract_fusion
  326.5 0.8 copy-done.1
  327.3 1.4 fusion.63
  328.7 0.3 all-gather.18.cloned.1.call-start
  329.3 1.3 fusion.15
  330.6 1.0 fusion.54
  331.6 1.9 convolution_subtract_fusion.3
  333.6 0.6 fusion.73
  334.2 2.1 convolution_add_fusion
  336.3 1.0 fusion.12
  337.3 1.7 fusion.65
  339.3 1.3 fusion.11
  340.6 1.0 fusion.49
  341.6 0.9 convolution_subtract_fusion.1
  342.6 1.0 fusion.8
  343.5 0.9 fusion.61
  344.6 0.3 while.6
  344.8 2.1 fusion.41
  347.1 16.9 %all-gather.16.cloned.1.call-done = f32[128,64,64]{2,1,0:T(8,128)} async-done(((f32[16,64,64]{2,1,0:T(8,128)}), f32[128,64,64]{2,1,0:T(8,128)}) %all-gather.16.cloned.1.call-update) | async-done | bytes 2097168 | tf_op jit(solution)/shard_map/all_gather | solution.py:11
  364.0 38.3 %all-gather.18.cloned.1.call-done = f32[128,64,64]{2,1,0:T(8,128)} async-done(((f32[16,64,64]{2,1,0:T(8,128)}), f32[128,64,64]{2,1,0:T(8,128)}) %all-gather.18.cloned.1.call-update) | async-done | bytes 2097168 | tf_op jit(solution)/shard_map/all_gather | solution.py:11
  402.5 1.0 multiply_reduce_fusion
  403.5 0.3 copy.132
  404.5 0.7 copy.134
  405.2 26.5 %all-to-all-start.2 = ((bf16[8,8,1024]{2,1,0:T(8,128)(2,1)}), bf16[8,8,1024]{2,1,0:T(8,128)(2,1)S(1)}, u32[]{:S(2)}, u32[]{:S(2)}) async-start(bf16[8,8,1024]{2,1,0:T(8,128)(2,1)} %copy.134), calls=%async_computation.2 | async-start | bytes 262144 | tf_op jit(solution)/shard_map/all_to_all | solution.py:192
  432.2 5.0 %all-to-all-done.2 = bf16[8,8,1024]{2,1,0:T(8,128)(2,1)S(1)} async-done(((bf16[8,8,1024]{2,1,0:T(8,128)(2,1)}), bf16[8,8,1024]{2,1,0:T(8,128)(2,1)S(1)}, u32[]{:S(2)}, u32[]{:S(2)}) %all-to-all-start.2) | async-done | bytes 131104 | tf_op jit(solution)/shard_map/all_to_all | solution.py:192
  437.2 0.7 fusion.56
  (92 shorter events, 4.3 us)
Async XLA Ops:
  6.5 15.9 %copy-start = (bf16[1,1,64,1024]{3,2,1,0:T(8,128)(2,1)S(1)}, bf16[1,1,64,1024]{3,2,1,0:T(8,128)(2,1)}, u32[]{:S(2)}) copy-start(bf16[1,1,64,1024]{3,2,1,0:T(8,128)(2,1)} %param.11) | copy-start | bytes 393220
  6.5 120.5 %all-gather.10.cloned.1.call-start = ((), (), s32[]{:S(2)}) async-start(), calls=%async_computation.3 | async-start | bytes 7864320 | tf_op jit(solution)/shard_map/all_gather | solution.py:157
  24.7 8.4 %all-to-all-start = ((bf16[8,2,128]{2,1,0:T(2,128)(2,1)}), bf16[8,2,128]{2,1,0:T(2,128)(2,1)S(1)}, u32[]{:S(2)}, u32[]{:S(2)}) async-start(bf16[8,2,128]{2,1,0:T(2,128)(2,1)} %reshape.328), calls=%async_computation | async-start | bytes 8192 | tf_op jit(solution)/shard_map/all_to_all | solution.py:179
  28.5 316.0 %all-gather.12.cloned.1.call-start = ((), (), s32[]{:S(2)}) async-start(), calls=%async_computation.4 | async-start | bytes 4718592 | tf_op jit(solution)/shard_map/all_gather | solution.py:11
  28.5 104.1 %copy-start.14 = (pred[64,64]{1,0:T(8,128)(4,1)}, pred[64,64]{1,0:T(8,128)(4,1)S(1)}, u32[]{:S(2)}) copy-start(pred[64,64]{1,0:T(8,128)(4,1)S(1)} %get-tuple-element.250) | copy-start | bytes 12292
  28.6 187.3 %copy-start.7 = (f32[64,64]{1,0:T(8,128)}, f32[64,64]{1,0:T(8,128)S(1)}, u32[]{:S(2)}) copy-start(f32[64,64]{1,0:T(8,128)S(1)} %get-tuple-element.251) | copy-start | bytes 49156
  28.6 104.0 %copy-start.19 = (pred[64,64]{1,0:T(8,128)(4,1)}, pred[64,64]{1,0:T(8,128)(4,1)S(1)}, u32[]{:S(2)}) copy-start(pred[64,64]{1,0:T(8,128)(4,1)S(1)} %get-tuple-element.248) | copy-start | bytes 12292
  28.7 104.1 %copy-start.20 = (pred[64,64]{1,0:T(8,128)(4,1)}, pred[64,64]{1,0:T(8,128)(4,1)S(1)}, u32[]{:S(2)}) copy-start(pred[64,64]{1,0:T(8,128)(4,1)S(1)} %get-tuple-element.249) | copy-start | bytes 12292
  28.7 104.0 %copy-start.13 = (f32[64,64]{1,0:T(8,128)}, f32[64,64]{1,0:T(8,128)S(1)}, u32[]{:S(2)}) copy-start(f32[64,64]{1,0:T(8,128)S(1)} %fusion.79) | copy-start | bytes 49156
  132.7 85.7 %copy-start.11 = (f32[64,16]{0,1:T(8,128)}, f32[64,16]{0,1:T(8,128)S(1)}, u32[]{:S(2)}) copy-start(f32[64,16]{0,1:T(8,128)S(1)} %add_sqrt_fusion.4) | copy-start | bytes 12292
  217.2 127.3 %all-gather.14.cloned.1.call-start = ((), (), s32[]{:S(2)}) async-start(), calls=%async_computation.5 | async-start | bytes 4718592 | tf_op jit(solution)/shard_map/all_gather | solution.py:11
  225.2 11.9 %all-to-all-start.1 = ((bf16[8,2,12288]{2,1,0:T(2,128)(2,1)}), bf16[8,2,12288]{2,1,0:T(2,128)(2,1)S(1)}, u32[]{:S(2)}, u32[]{:S(2)}) async-start(bf16[8,2,12288]{2,1,0:T(2,128)(2,1)} %reshape.330), calls=%async_computation.1 | async-start | bytes 786432 | tf_op jit(solution)/shard_map/all_to_all | solution.py:172
  228.8 135.2 %all-gather.16.cloned.1.call-start = ((), (), s32[]{:S(2)}) async-start(), calls=%async_computation.6 | async-start | bytes 4718592 | tf_op jit(solution)/shard_map/all_gather | solution.py:11
  240.5 81.8 %copy-start.6 = (f32[64,1,16,64]{3,2,1,0:T(8,128)S(1)}, f32[64,1,16,64]{3,2,1,0:T(8,128)}, u32[]{:S(2)}) copy-start(f32[64,1,16,64]{3,2,1,0:T(8,128)} %get-tuple-element.220) | copy-start | bytes 786436
  240.5 81.8 %copy-start.9 = (f32[16,64]{1,0:T(8,128)S(1)}, f32[16,64]{1,0:T(8,128)}, u32[]{:S(2)}) copy-start(f32[16,64]{1,0:T(8,128)} %get-tuple-element.234) | copy-start | bytes 12292
  240.5 81.8 %copy-start.10 = (f32[16,64]{1,0:T(8,128)S(1)}, f32[16,64]{1,0:T(8,128)}, u32[]{:S(2)}) copy-start(f32[16,64]{1,0:T(8,128)} %get-tuple-element.235) | copy-start | bytes 12292
  240.5 84.5 %copy-start.8 = (f32[64,64]{1,0:T(8,128)S(1)}, f32[64,64]{1,0:T(8,128)}, u32[]{:S(2)}) copy-start(f32[64,64]{1,0:T(8,128)} %copy-done.7) | copy-start | bytes 49156
  240.5 84.5 %copy-start.17 = (f32[16,64]{1,0:T(8,128)S(1)}, f32[16,64]{1,0:T(8,128)}, u32[]{:S(2)}) copy-start(f32[16,64]{1,0:T(8,128)} %get-tuple-element.233) | copy-start | bytes 12292
  240.5 84.5 %copy-start.21 = (f32[16]{0:T(128)S(1)}, f32[16]{0:T(128)}, u32[]{:S(2)}) copy-start(f32[16]{0:T(128)} %exp.84) | copy-start | bytes 196
  243.0 86.0 %copy-start.3 = (f32[64,1,16,64]{3,2,1,0:T(8,128)S(1)}, f32[64,1,16,64]{3,2,1,0:T(8,128)}, u32[]{:S(2)}) copy-start(f32[64,1,16,64]{3,2,1,0:T(8,128)} %get-tuple-element.225) | copy-start | bytes 786436
  322.3 6.9 %copy-start.12 = (f32[64,16]{0,1:T(8,128)S(1)}, f32[64,16]{0,1:T(8,128)}, u32[]{:S(2)}) copy-start(f32[64,16]{0,1:T(8,128)} %copy-done.11) | copy-start | bytes 12292
  322.3 6.9 %copy-start.15 = (pred[64,64]{1,0:T(8,128)(4,1)S(1)}, pred[64,64]{1,0:T(8,128)(4,1)}, u32[]{:S(2)}) copy-start(pred[64,64]{1,0:T(8,128)(4,1)} %copy-done.14) | copy-start | bytes 12292
  326.5 0.8 copy-start.1
  327.3 4.3 copy-start.18
  328.7 73.7 %all-gather.18.cloned.1.call-start = ((), (), s32[]{:S(2)}) async-start(), calls=%async_computation.7 | async-start | bytes 4718592 | tf_op jit(solution)/shard_map/all_gather | solution.py:11
  329.3 4.3 copy-start.2
  333.6 5.4 %copy-start.4 = (f32[64,1,16,64]{3,2,1,0:T(8,128)S(1)}, f32[64,1,16,64]{3,2,1,0:T(8,128)}, u32[]{:S(2)}) copy-start(f32[64,1,16,64]{3,2,1,0:T(8,128)} %get-tuple-element.222) | copy-start | bytes 786436
  337.3 4.4 copy-start.5
  337.3 4.4 copy-start.16
  405.2 32.0 %all-to-all-start.2 = ((bf16[8,8,1024]{2,1,0:T(8,128)(2,1)}), bf16[8,8,1024]{2,1,0:T(8,128)(2,1)S(1)}, u32[]{:S(2)}, u32[]{:S(2)}) async-start(bf16[8,8,1024]{2,1,0:T(8,128)(2,1)} %copy.134), calls=%async_computation.2 | async-start | bytes 262144 | tf_op jit(solution)/shard_map/all_to_all | solution.py:192
Sparse Core Ops, SparseCore 0:
  8.9 118.0 all-gather.9
  217.4 39.3 all-gather.11
  258.6 37.0 all-gather.13
  328.8 35.1 all-gather.15
  365.8 36.5 all-gather.17
where the time goes:
time: 453 us; the launch traced here: 445 us
  other arithmetic  168 us (37%)
  waiting for transfers between devices  164 us (36%)
  matrix products  37.2 us (8%)
  starting transfers between devices  35 us (8%)
  blocking collectives  15.1 us (3%)
  between operations  14.1 us (3%)
  local copies, waits for them, and re-layouts  11.5 us (3%)
    another operation x5, other arithmetic, group_terms(): lax.linalg.triangular_solve(system, jnp.concatenate([rhs_values, rhs_keys...  158 us
    all_gather x1, waiting for transfers between devices, on_device(): lax.all_gather(w_qkv, 'face', axis=1, tiled=True)  91.3 us
    all_gather x4, waiting for transfers between devices, carried_in(): gathered = jax.tree.map(lambda a: lax.all_gather(a, axis), part)  55.3 us
    all_to_all x1, starting transfers between devices, on_device(): lax.all_to_all(col_tall, 'strip', split_axis=0, concat_axis=1, tiled=True)  26.5 us
    all_gather x1, blocking collectives, on_device(): lax.all_gather(w_gate, 'face', axis=1, tiled=True)  15.1 us
  transfers between devices with their start and end apart: 8, of which 6 were waited for; matrix products, arithmetic and copies ran while one was open for 27% of the time, Pallas kernels for 0%

commit v1 on v0

v1 whole, which is shorter than its diff:
```python
import functools

import jax
import jax.numpy as jnp
from jax import lax
from jax.experimental import pallas as pl
from jax.experimental.pallas import tpu as pltpu
from jax.sharding import PartitionSpec as P

MESH = pl.DeviceIdType.MESH
f32 = jnp.float32
bf16 = jnp.bfloat16


def greet_all(faces, strips, me_f, me_s):
    barrier = pltpu.get_barrier_semaphore()
    total = faces * strips
    me = me_f * strips + me_s

    def one(step, carry):
        other = lax.rem(me + step, total)
        pl.semaphore_signal(
            barrier,
            inc=1,
            device_id=(other // strips, lax.rem(other, strips)),
            device_id_type=MESH,
        )
        return carry

    lax.fori_loop(1, total, one, 0)
    pl.semaphore_wait(barrier, total - 1)


def project_kernel(
    cfg, px_ref, wq_ref, wg_ref, slabs_ref, gates_ref,
    px_all, proj, glog, px_send, px_recv, slab_send, slab_recv, gate_send, gate_recv,
):
    faces, strips, groups, rep, heads, per_group = cfg
    me_f, me_s = lax.axis_index("face"), lax.axis_index("strip")
    n_slab = proj.shape[1]
    gate_cols = wg_ref.shape[1]
    width = proj.shape[3]
    n_gate = gate_cols // per_group
    greet_all(faces, strips, me_f, me_s)

    def px_copy(step):
        face = lax.rem(me_f + step, faces)
        return pltpu.make_async_remote_copy(
            src_ref=px_ref,
            dst_ref=px_all.at[me_f],
            send_sem=px_send.at[step],
            recv_sem=px_recv.at[me_f],
            device_id=(face, me_s),
            device_id_type=MESH,
        )

    for step in range(1, faces):
        px_copy(step).start()

    def slab_copy(step, j, r):
        face = lax.rem(me_f + step, faces)
        slab = me_f * n_slab + j
        kind, group = slab // groups, lax.rem(slab, groups)
        dest = group * rep + r
        remote = pltpu.make_async_remote_copy(
            src_ref=proj.at[step, j],
            dst_ref=slabs_ref.at[kind, me_s],
            send_sem=slab_send.at[step, j, r],
            recv_sem=slab_recv.at[kind, me_s],
            device_id=(face, dest),
            device_id_type=MESH,
        )
        local = pltpu.make_async_copy(
            proj.at[step, j], slabs_ref.at[kind, me_s], slab_recv.at[kind, me_s]
        )
        return remote, local, dest

    def gate_copy(step, i, r):
        face = lax.rem(me_f + step, faces)
        first = me_f * gate_cols
        kind, group = first // heads, lax.rem(first, heads) // per_group + i
        dest = group * rep + r
        remote = pltpu.make_async_remote_copy(
            src_ref=glog.at[step],
            dst_ref=gates_ref.at[kind, me_s],
            send_sem=gate_send.at[step, i, r],
            recv_sem=gate_recv.at[kind, me_s],
            device_id=(face, dest),
            device_id_type=MESH,
        )
        local = pltpu.make_async_copy(
            glog.at[step], gates_ref.at[kind, me_s], gate_recv.at[kind, me_s]
        )
        return remote, local, dest

    def launch(copies, step):
        remote, local, dest = copies
        if step == 0:
            pl.when(dest == me_s)(local.start)
            pl.when(dest != me_s)(remote.start)
        else:
            remote.start()

    def drain(copies, step):
        remote, _, dest = copies
        if step == 0:
            pl.when(dest != me_s)(remote.wait_send)
        else:
            remote.wait_send()

    for step in range(faces):
        if step == 0:
            px = px_ref[...]
        else:
            face = lax.rem(me_f + step, faces)
            pltpu.make_async_copy(px_ref, px_all.at[face], px_recv.at[face]).wait()
            px = px_all[face]
        logits = jnp.dot(px, wg_ref[...], preferred_element_type=f32)
        glog[step] = logits.astype(bf16).astype(f32).T
        for i in range(n_gate):
            for r in range(rep):
                launch(gate_copy(step, i, r), step)
        for j in range(n_slab):
            proj[step, j] = jnp.dot(
                px, wq_ref[:, j * width : (j + 1) * width], preferred_element_type=f32
            ).astype(bf16)
        for j in range(n_slab):
            for r in range(rep):
                launch(slab_copy(step, j, r), step)

    for step in range(1, faces):
        px_copy(step).wait_send()
    for step in range(faces):
        for i in range(n_gate):
            for r in range(rep):
                drain(gate_copy(step, i, r), step)
        for j in range(n_slab):
            for r in range(rep):
                drain(slab_copy(step, j, r), step)
    for source in range(strips):
        for kind in range(slabs_ref.shape[0]):
            pltpu.make_async_copy(
                proj.at[0, 0], slabs_ref.at[kind, source], slab_recv.at[kind, source]
            ).wait()
        for kind in range(gates_ref.shape[0]):
            pltpu.make_async_copy(
                glog.at[0], gates_ref.at[kind, source], gate_recv.at[kind, source]
            ).wait()


def mm(a, b, dims=((1,), (0,))):
    return lax.dot_general(
        a.astype(bf16), b.astype(bf16), (dims, ((), ())), preferred_element_type=f32
    )


def split_mm(exact, wide, pieces):
    exact = exact.astype(bf16)
    total, rest = None, wide
    for _ in range(pieces):
        piece = rest.astype(bf16)
        rest = rest - piece.astype(f32)
        term = jnp.dot(exact, piece, preferred_element_type=f32)
        total = term if total is None else total + term
    return total


def mm_split(wide, exact, pieces):
    exact = exact.astype(bf16)
    total, rest = None, wide
    for _ in range(pieces):
        piece = rest.astype(bf16)
        rest = rest - piece.astype(f32)
        term = jnp.dot(piece, exact, preferred_element_type=f32)
        total = term if total is None else total + term
    return total


def scan_kernel(
    cfg, first_ref, slabs_ref, gates_ref, rate_ref, bias_ref, out_ref,
    feats, gates, row_buf, col_buf, states,
):
    chunk, per_group, tall, wide, dk = cfg
    strips, block, width = slabs_ref.shape[1:]
    count = strips * block
    first = first_ref[0]
    gate_cols = gates_ref.shape[2]

    lane = lax.broadcasted_iota(jnp.int32, (width, width), 1)
    sub = lax.broadcasted_iota(jnp.int32, (width, width), 0)
    same_head = (lane // dk) == (sub // dk)
    head_ones = same_head.astype(f32)
    ti = lax.broadcasted_iota(jnp.int32, (chunk, chunk), 0)
    tj = lax.broadcasted_iota(jnp.int32, (chunk, chunk), 1)
    inclusive = ti >= tj
    tri = inclusive.astype(f32)
    eye = (ti == tj).astype(f32)

    def prepare(s, carry):
        at = pl.ds(s * block, block)
        for kind in range(3):
            x = slabs_ref[kind, s].astype(f32)
            if kind < 2:
                x = x * lax.rsqrt(mm_split(x * x, head_ones, 2) + 1e-06)
            feats[kind, at, :] = x
        for a in range(per_group):
            head = first + a
            row = lax.rem(head, gate_cols)
            decay = -rate_ref[head] * jnp.exp(gates_ref[0, s, pl.ds(row, 1), :])
            strength = jax.nn.sigmoid(gates_ref[1, s, pl.ds(row, 1), :] + bias_ref[head])
            gates[a, at, :] = jnp.broadcast_to(decay, (chunk, block)).T
            gates[per_group + a, at, :] = jnp.broadcast_to(strength, (chunk, block)).T
        return carry

    lax.fori_loop(0, strips, prepare, 0, unroll=True if strips <= 8 else 1)

    columns = chunk // tall
    flane = lax.broadcasted_iota(jnp.int32, (chunk, width), 1) // dk

    def lanes_of(parts):
        out = parts[0][:, :width]
        for a in range(1, per_group):
            out = jnp.where(flane == a, parts[a][:, :width], out)
        return out

    def stacked(x):
        if per_group == 1:
            return x
        return jnp.concatenate(
            [jnp.where(flane == a, x, jnp.zeros_like(x)) for a in range(per_group)], axis=0
        )

    def side_by_side(parts):
        return parts[0] if per_group == 1 else jnp.concatenate(parts, axis=1)

    def load(ref, which, i, by_column):
        if not by_column:
            return ref[which, pl.ds(pl.multiple_of(i * chunk, chunk), chunk), :]
        return jnp.concatenate(
            [ref[which, pl.ds(i * columns + c, tall, stride=wide), :] for c in range(columns)],
            axis=0,
        )

    states[...] = jnp.zeros_like(states)

    def advance(i, carry):
        work = []
        for order in range(2):
            q, k, v = (load(feats, kind, i, order) for kind in range(3))
            cums, betas, systems, scores = [], [], [], []
            for a in range(per_group):
                cum = split_mm(tri, load(gates, a, i, order), 3)
                beta = load(gates, per_group + a, i, order)
                gap = cum - cum.T
                within = jnp.where(inclusive, jnp.exp(jnp.where(inclusive, gap, 0.0)), 0.0)
                k_a = k if per_group == 1 else jnp.where(flane == a, k, 0.0)
                q_a = q if per_group == 1 else jnp.where(flane == a, q, 0.0)
                dots = mm(jnp.concatenate([k_a, q_a], axis=0), k, ((1,), (1,)))
                systems.append(within * dots[:chunk] * beta)
                scores.append(within * dots[chunk:])
                cums.append(cum)
                betas.append(beta)
            work.append((q, k, v, cums, betas, systems, scores))

        inverses = [[None] * per_group for _ in range(2)]
        half = 1
        while half < chunk:
            here = ((ti // (2 * half)) == (tj // (2 * half))) & (
                (lax.rem(ti, 2 * half) >= half) & (lax.rem(tj, 2 * half) < half)
            )
            lows = [
                [jnp.where(here, work[o][5][a], 0.0) for a in range(per_group)] for o in range(2)
            ]
            if half == 1:
                inverses = [[eye - low for low in row] for row in lows]
            else:
                firsts = [
                    [mm(lows[o][a], inverses[o][a]) for a in range(per_group)] for o in range(2)
                ]
                inverses = [
                    [inverses[o][a] - mm(inverses[o][a], firsts[o][a]) for a in range(per_group)]
                    for o in range(2)
                ]
            half *= 2

        for order in range(2):
            q, k, v, cums, betas, _, scores = work[order]
            beta = lanes_of(betas)
            cum = lanes_of(cums)
            scale = jnp.exp(cum)
            last = cum[chunk - 1 : chunk, :]
            tail = jnp.exp(last - cum)
            both = side_by_side(inverses[order])
            u = mm(both, stacked(v * beta))
            w = mm(both, stacked(k * (beta * scale)))
            state = states[order]
            fresh = u - mm(w, state)
            out = mm(q * scale, state) + mm(side_by_side(scores), stacked(fresh))
            grown = mm(k * tail, fresh, ((0,), (0,)))
            decayed = state * jnp.exp(last)
            states[order] = decayed + jnp.where(same_head, grown, 0.0)
            normed = out * lax.rsqrt(mm_split(out * out, head_ones, 2) * (1.0 / dk) + 1e-06)
            if order == 0:
                row_buf[pl.ds(pl.multiple_of(i * chunk, chunk), chunk), :] = normed
            else:
                normed = normed.astype(bf16).astype(f32)
                for c in range(columns):
                    col_buf[pl.ds(i * columns + c, tall, stride=wide), :] = normed[
                        c * tall : (c + 1) * tall
                    ]
        return carry

    lax.fori_loop(0, count // chunk, advance, 0)

    def finish(s, carry):
        at = pl.ds(s * block, block)
        out_ref[s] = (row_buf[at, :] + col_buf[at, :]).astype(bf16)
        return carry

    lax.fori_loop(0, strips, finish, 0)


def return_kernel(faces, strips, mixed_ref, out_ref, send_sem, recv_sem):
    me_f, me_s = lax.axis_index("face"), lax.axis_index("strip")
    barrier = pltpu.get_barrier_semaphore()
    for step in range(1, strips):
        pl.semaphore_signal(
            barrier, inc=1, device_id=(me_f, lax.rem(me_s + step, strips)), device_id_type=MESH
        )
    pl.semaphore_wait(barrier, strips - 1)

    def copy(step):
        dest = lax.rem(me_s + step, strips)
        return pltpu.make_async_remote_copy(
            src_ref=mixed_ref.at[dest],
            dst_ref=out_ref.at[me_s],
            send_sem=send_sem.at[step],
            recv_sem=recv_sem.at[me_s],
            device_id=(me_f, dest),
            device_id_type=MESH,
        )

    for step in range(1, strips):
        copy(step).start()
    own = pltpu.make_async_copy(mixed_ref.at[me_s], out_ref.at[me_s], recv_sem.at[me_s])
    own.start()
    for step in range(1, strips):
        copy(step).wait_send()
    for source in range(strips):
        pltpu.make_async_copy(
            mixed_ref.at[0], out_ref.at[source], recv_sem.at[source]
        ).wait()


def scan_call(first, slabs, gates, decay_rate, beta_bias, per_group, tall, wide, dk):
    strips, block, width = slabs.shape[1:]
    count = strips * block
    chunk = min(128, count)
    vmem = pl.BlockSpec(memory_space=pltpu.VMEM)
    smem = pl.BlockSpec(memory_space=pltpu.SMEM)
    return pl.pallas_call(
        functools.partial(scan_kernel, (chunk, per_group, tall, wide, dk)),
        out_shape=jax.ShapeDtypeStruct((strips, block, width), bf16),
        in_specs=[smem, vmem, vmem, smem, smem],
        out_specs=vmem,
        scratch_shapes=[
            pltpu.VMEM((3, count, width), f32),
            pltpu.VMEM((2 * per_group, count, chunk), f32),
            pltpu.VMEM((count, width), f32),
            pltpu.VMEM((count, width), f32),
            pltpu.VMEM((2, width, width), f32),
        ],
        name="scans",
    )(first, slabs, gates, decay_rate, beta_bias)


def on_device(faces, strips, pixels_in, w_qkv, w_gate, decay_rate, beta_bias):
    _, rows_here, wide, features = pixels_in.shape
    heads = decay_rate.shape[0]
    block = rows_here * wide
    tall = rows_here * strips
    model = w_qkv.shape[1] * faces // 3
    dk = model // heads
    groups = min(strips, heads)
    rep = strips // groups
    per_group = heads // groups
    width = per_group * dk
    n_slab = w_qkv.shape[1] // width
    gate_cols = w_gate.shape[1]
    n_gate = gate_cols // per_group
    vmem = pl.BlockSpec(memory_space=pltpu.VMEM)
    dma = pltpu.SemaphoreType.DMA
    slabs, gates = pl.pallas_call(
        functools.partial(project_kernel, (faces, strips, groups, rep, heads, per_group)),
        out_shape=(
            jax.ShapeDtypeStruct((3, strips, block, width), bf16),
            jax.ShapeDtypeStruct((2, strips, gate_cols, block), f32),
        ),
        in_specs=[vmem, vmem, vmem],
        out_specs=(vmem, vmem),
        scratch_shapes=[
            pltpu.VMEM((faces, block, features), bf16),
            pltpu.VMEM((faces, n_slab, block, width), bf16),
            pltpu.VMEM((faces, gate_cols, block), f32),
            dma((faces,)),
            dma((faces,)),
            dma((faces, n_slab, rep)),
            dma((3, strips)),
            dma((faces, n_gate, rep)),
            dma((2, strips)),
        ],
        compiler_params=pltpu.CompilerParams(collective_id=0, has_side_effects=True),
        name="project",
    )(pixels_in.reshape(block, features), w_qkv, w_gate)
    first = (lax.axis_index("strip") // rep * per_group).astype(jnp.int32).reshape(1)
    mixed = scan_call(first, slabs, gates, decay_rate, beta_bias, per_group, tall, wide, dk)
    returned = pl.pallas_call(
        functools.partial(return_kernel, faces, strips),
        out_shape=jax.ShapeDtypeStruct((strips, block, width), bf16),
        in_specs=[vmem],
        out_specs=vmem,
        scratch_shapes=[dma((strips,)), dma((strips,))],
        compiler_params=pltpu.CompilerParams(collective_id=1, has_side_effects=True),
        name="give_back",
    )(mixed)
    whole = returned[::rep].transpose(1, 0, 2)
    return whole.reshape(1, rows_here, wide, model)


def solution(mesh):
    in_specs = (P("face", "strip", None, None), P(None, "face"), P(None, "face"), P(), P())
    out_specs = P("face", "strip", None, None)
    return jax.shard_map(
        functools.partial(on_device, mesh.shape["face"], mesh.shape["strip"]),
        mesh=mesh,
        in_specs=in_specs,
        out_specs=out_specs,
        check_vma=False,
    )
```

time: 453 us -> 55.7 us (0.12); the launches traced: 445 us -> 54.7 us
  other arithmetic: 168 us -> 0 us
  waiting for transfers between devices: 164 us -> 0 us
  Pallas kernels: 0 us -> 51.4 us
  matrix products: 37.2 us -> 0 us
  starting transfers between devices: 35 us -> 0 us
  blocking collectives: 15.1 us -> 0 us
  between operations: 14.1 us -> 0.02 us
  local copies, waits for them, and re-layouts: 11.5 us -> 3.28 us
    another operation x7 -> x0, other arithmetic: 158 us -> none  [the longest x5 158 us: group_terms(): lax.linalg.triangular_solve(system, jnp.concatenate([rhs_values, rhs_keys...]
    all_gather x5 -> x0, waiting for transfers between devices: 147 us -> none  [the longest x1 91.3 us: on_device(): lax.all_gather(w_qkv, 'face', axis=1, tiled=True)]
    pallas_call x0 -> x3, Pallas kernels: none -> 51.4 us  [the longest x1 30.1 us: on_device(): pl.pallas_call(functools.partial(project_kernel, (faces, strips, groups,...]
    dot_general x24 -> x0, matrix products: 33.9 us -> none  [the longest x2 4.19 us: group_terms(): jnp.einsum('hcv,hck->hvk', new_values, weighted_keys, precision=highest)]
    all_to_all x3 -> x0, starting transfers between devices: 33.9 us -> none  [the longest x1 26.5 us: on_device(): lax.all_to_all(col_tall, 'strip', split_axis=0, concat_axis=1, tiled=True)]
    all_to_all x3 -> x0, waiting for transfers between devices: 16.3 us -> none  [the longest x1 7.49 us: on_device(): lax.all_to_all(projected.reshape(rows_here, width_cols, -1), 'strip', spl...]
    all_gather x1 -> x0, blocking collectives: 15.1 us -> none  [on_device(): lax.all_gather(w_gate, 'face', axis=1, tiled=True)]
  transfers between devices with their start and end apart: 8 -> 0, of which waited for: 6 -> 0; matrix products, arithmetic and copies ran while one was open for 27% -> 0% of each run, Pallas kernels for 0% -> 0%
where the time goes in v1:
time: 55.7 us; the launch traced here: 54.7 us
  Pallas kernels  51.4 us (92%)
  local copies, waits for them, and re-layouts  3.28 us (6%)
    pallas_call x1, Pallas kernels, on_device(): pl.pallas_call(functools.partial(project_kernel, (faces, strips, groups,...  30.1 us
    pallas_call x1, Pallas kernels, scan_call(): pl.pallas_call(functools.partial(scan_kernel, (chunk, per_group, tall, wi...  14.8 us
    pallas_call x1, Pallas kernels, on_device(): pl.pallas_call(functools.partial(return_kernel, faces, strips), out_shape...  6.47 us
    unnamed x1, local copies, waits for them, and re-layouts  1.57 us

profile of v1, /device:TPU:0, one launch (start us, length us, event | category | flops | bytes accessed | tf_op | source)
XLA Modules:
  0.0 54.7 jit_solution(12018453262798723342)
XLA Ops:
  0.0 1.6 %copy.7.wg_ref = bf16[1024,8]{1,0:T(8,128)(2,1)} copy(bf16[1024,8]{0,1:T(8,128)(2,1)} %param.7) | data formatting | bytes 32768 | tf_op args[2]
  1.6 30.1 %project.1 = (bf16[3,8,64,128]{3,2,1,0:T(8,128)(2,1)}, f32[2,8,8,64]{3,2,1,0:T(8,128)}) custom-call(bf16[64,1024]{1,0:T(8,128)(2,1)} %bitcast.4, bf16[1024,768]{1,0:T(8,128)(2,1)} %wq_ref.1, bf16[1024,8]{1,0:T(8,128)(2,1)} %copy.7.wg_ref), custom_call_target="tpu_custom_call" | custom-call | tf_op jit(solution)/shard_map/project/pallas_call | solution.py:393
  31.7 14.8 %scans.1.mixed_ref = bf16[8,64,128]{2,1,0:T(8,128)(2,1)} custom-call(s32[1]{0:T(128)} %bitcast.first_ref, bf16[3,8,64,128]{3,2,1,0:T(8,128)(2,1)} %get-tuple-element.7.slabs_ref, f32[2,8,8,64]{3,2,1,0:T(8,128)} %get-tuple-element.8.gates_ref, f32[16]{0:T(128)} %rate_ref.1, f32[16]{0:T(128)} %bias_ref.1), custom_call_target="tpu_custom_call" | custom-call | tf_op jit(solution)/shard_map/scans/pallas_call | solution.py:361
  46.5 6.5 %give_back.1 = bf16[8,64,128]{2,1,0:T(8,128)(2,1)} custom-call(bf16[8,64,128]{2,1,0:T(8,128)(2,1)} %scans.1.mixed_ref), custom_call_target="tpu_custom_call" | custom-call | tf_op jit(solution)/shard_map/give_back/pallas_call | solution.py:417
  53.0 1.0 %copy.8 = bf16[64,8,128]{2,1,0:T(8,128)(2,1)S(1)} copy(bf16[64,8,128]{2,0,1:T(8,128)(2,1)} %bitcast.3) | data formatting | bytes 262144 | tf_op jit(solution)/shard_map/transpose | solution.py:426
  54.0 0.7 %reshape.11 = bf16[1,1,64,1024]{3,2,1,0:T(8,128)(2,1)} reshape(bf16[64,8,128]{2,1,0:T(8,128)(2,1)S(1)} %copy.8) | data formatting | bytes 262144 | tf_op jit(solution)/shard_map/reshape | solution.py:427

commit v2 on v1

v2 whole, which is shorter than its diff:
```python
import functools

import jax
import jax.numpy as jnp
from jax import lax
from jax.experimental import pallas as pl
from jax.experimental.pallas import tpu as pltpu
from jax.sharding import PartitionSpec as P

MESH = pl.DeviceIdType.MESH
f32 = jnp.float32
bf16 = jnp.bfloat16


def group_of(place, strips, groups):
    rep = strips // groups
    if rep > 1 or groups % 2:
        return place // rep
    return jnp.where(lax.rem(place, 2) == 0, place // 2, groups - 1 - place // 2)


def project_kernel(
    cfg, px_ref, wq_ref, wg_ref, slabs_ref, gates_ref,
    px_all, wbuf, wg_own, wg_all, acc, px_send, px_fwd, px_recv, w_send, w_recv, g_send, g_recv,
):
    faces, strips, groups, n_slab, pieces = cfg
    me_f, me_s = lax.axis_index("face"), lax.axis_index("strip")
    block, features = px_ref.shape
    count = strips * block
    width = wbuf.shape[2]
    chips = strips // 2
    core, chip = lax.rem(me_s, 2), me_s // 2
    partner = chip * 2 + (1 - core)
    group = group_of(me_s, strips, groups)
    depth = features // pieces

    def chip_at(step):
        return lax.rem(chip + step, chips) * 2 + core

    barrier = pltpu.get_barrier_semaphore()

    def greet(face, strip):
        pl.semaphore_signal(barrier, inc=1, device_id=(face, strip), device_id_type=MESH)

    greet(me_f, partner)
    for step in range(1, chips):
        greet(me_f, chip_at(step))
    for step in range(1, faces):
        greet(lax.rem(me_f + step, faces), me_s)

    wg_own[...] = wg_ref[...].astype(f32)

    def rows_of(strip):
        return px_all.at[pl.ds(pl.multiple_of(strip * block, block), block)]

    own_px = pltpu.make_async_copy(px_ref, rows_of(me_s), px_recv.at[me_s])
    own_px.start()
    pl.semaphore_wait(barrier, 1 + chips - 1 + faces - 1)

    def weight_from(kind):
        slab = kind * groups + group
        return slab // n_slab, lax.rem(slab, n_slab)

    def weight_src(j, p):
        rows = pl.ds(p * depth, depth)
        if len(wq_ref.shape) == 3:
            return wq_ref.at[j, rows]
        return wq_ref.at[rows, pl.ds(pl.multiple_of(j * width, width), width)]

    def weight_copy(kind, p, src, side):
        return pltpu.make_async_remote_copy(
            src_ref=src,
            dst_ref=wbuf.at[kind, pl.ds(p * depth, depth)],
            send_sem=w_send.at[kind, p, side],
            recv_sem=w_recv.at[kind, p],
            device_id=(me_f + (1 if side else -1), me_s),
            device_id_type=MESH,
        )

    def own_weight(kind, p, j):
        return pltpu.make_async_copy(
            weight_src(j, p), wbuf.at[kind, pl.ds(p * depth, depth)], w_recv.at[kind, p]
        )

    for p in range(pieces):
        for kind in range(3):
            owner, j = weight_from(kind)

            @pl.when(owner == me_f)
            def _(kind=kind, p=p, j=j):
                pl.when(me_f + 1 < faces)(weight_copy(kind, p, weight_src(j, p), 1).start)
                pl.when(me_f > 0)(weight_copy(kind, p, weight_src(j, p), 0).start)
                own_weight(kind, p, j).start()

    def px_copy(dest, sem, source, src):
        return pltpu.make_async_remote_copy(
            src_ref=src,
            dst_ref=rows_of(source),
            send_sem=sem,
            recv_sem=px_recv.at[source],
            device_id=(me_f, dest),
            device_id_type=MESH,
        )

    def px_out(step):
        return px_copy(chip_at(step), px_send.at[step], me_s, px_ref)

    def px_pass(step):
        source = chip_at(step)
        return px_copy(partner, px_fwd.at[step], source, rows_of(source))

    to_partner = px_copy(partner, px_send.at[0], me_s, px_ref)
    for step in range(1, chips):
        px_out(step).start()
    to_partner.start()

    def gate_copy(step):
        return pltpu.make_async_remote_copy(
            src_ref=wg_own,
            dst_ref=wg_all.at[me_f],
            send_sem=g_send.at[step],
            recv_sem=g_recv.at[me_f],
            device_id=(lax.rem(me_f + step, faces), me_s),
            device_id_type=MESH,
        )

    for step in range(1, faces):
        gate_copy(step).start()
    own_gate = pltpu.make_async_copy(wg_own, wg_all.at[me_f], g_recv.at[me_f])
    own_gate.start()

    def px_wait(strip):
        pltpu.make_async_copy(px_ref, rows_of(strip), px_recv.at[strip]).wait()

    def pass_pixels(step):
        px_wait(chip_at(step))
        px_pass(step).start()

    def pass_weights(p):
        for kind in range(3):
            owner, _ = weight_from(kind)
            here = wbuf.at[kind, pl.ds(p * depth, depth)]
            pltpu.make_async_copy(here, here, w_recv.at[kind, p]).wait()
            pl.when((owner < me_f) & (me_f + 1 < faces))(weight_copy(kind, p, here, 1).start)
            pl.when((owner > me_f) & (me_f > 0))(weight_copy(kind, p, here, 0).start)

    tile = min(512, count)

    def each_tile(body):
        if count == tile:
            body(pl.ds(0, tile), 0)
        else:

            def one(i, carry):
                body(pl.ds(pl.multiple_of(i * tile, tile), tile), i)
                return carry

            lax.fori_loop(0, count // tile, one, 0)

    def multiply(p):
        rows = pl.ds(p * depth, depth)
        weights = jnp.concatenate([wbuf[kind, rows, :] for kind in range(3)], axis=1)

        def body(at, _):
            term = jnp.dot(px_all[at, rows], weights, preferred_element_type=f32)
            if p > 0:
                term = term + acc[at, :]
            if p < pieces - 1:
                acc[at, :] = term
            else:
                for kind in range(3):
                    slabs_ref[kind, at, :] = term[
                        :, kind * width : (kind + 1) * width
                    ].astype(bf16)

        each_tile(body)

    for turn in range(max(pieces - 1, chips - 1)):
        if turn < pieces - 1:
            pass_weights(turn)
        if turn < chips - 1:
            pass_pixels(turn + 1)
    px_wait(me_s)
    px_wait(partner)
    for step in range(1, chips):
        px_wait(lax.rem(chip + step, chips) * 2 + (1 - core))
    for face in range(faces):
        pltpu.make_async_copy(wg_own, wg_all.at[face], g_recv.at[face]).wait()
    gate_w = jnp.concatenate([wg_all[face] for face in range(faces)], axis=0).astype(bf16)

    chunk = gates_ref.shape[2]

    def gate_body(at, i):
        logits = lax.dot_general(
            gate_w, px_all[at, :], (((1,), (1,)), ((), ())), preferred_element_type=f32
        )
        logits = logits.astype(bf16).astype(f32)
        for c in range(tile // chunk):
            gates_ref[i * (tile // chunk) + c] = logits[:, c * chunk : (c + 1) * chunk]

    each_tile(gate_body)
    for p in range(pieces - 1):
        multiply(p)
    pass_weights(pieces - 1)
    multiply(pieces - 1)

    to_partner.wait_send()
    for step in range(1, chips):
        px_out(step).wait_send()
        px_pass(step).wait_send()
    for step in range(1, faces):
        gate_copy(step).wait_send()
    for p in range(pieces):
        for kind in range(3):
            owner, _ = weight_from(kind)
            here = wbuf.at[kind, pl.ds(p * depth, depth)]
            pl.when((owner <= me_f) & (me_f + 1 < faces))(
                weight_copy(kind, p, here, 1).wait_send
            )
            pl.when((owner >= me_f) & (me_f > 0))(weight_copy(kind, p, here, 0).wait_send)


def mm(a, b, dims=((1,), (0,))):
    return lax.dot_general(
        a.astype(bf16), b.astype(bf16), (dims, ((), ())), preferred_element_type=f32
    )


def split_mm(exact, wide, pieces):
    exact = exact.astype(bf16)
    total, rest = None, wide
    for _ in range(pieces):
        piece = rest.astype(bf16)
        rest = rest - piece.astype(f32)
        term = jnp.dot(exact, piece, preferred_element_type=f32)
        total = term if total is None else total + term
    return total


def mm_split(wide, exact, pieces):
    exact = exact.astype(bf16)
    total, rest = None, wide
    for _ in range(pieces):
        piece = rest.astype(bf16)
        rest = rest - piece.astype(f32)
        term = jnp.dot(piece, exact, preferred_element_type=f32)
        total = term if total is None else total + term
    return total


def scan_kernel(
    cfg, first_ref, slabs_ref, gates_ref, rate_ref, bias_ref, out_ref,
    feats, gates, row_buf, col_buf, states,
):
    chunk, per_group, tall, wide, dk = cfg
    count, width = slabs_ref.shape[1:]
    strips, block, _ = out_ref.shape
    heads = gates_ref.shape[1] // 2
    first = first_ref[0]

    lane = lax.broadcasted_iota(jnp.int32, (width, width), 1)
    sub = lax.broadcasted_iota(jnp.int32, (width, width), 0)
    same_head = (lane // dk) == (sub // dk)
    head_ones = same_head.astype(f32)
    ti = lax.broadcasted_iota(jnp.int32, (chunk, chunk), 0)
    tj = lax.broadcasted_iota(jnp.int32, (chunk, chunk), 1)
    inclusive = ti >= tj
    tri = inclusive.astype(f32)
    eye = (ti == tj).astype(f32)

    def prepare(i, carry):
        at = pl.ds(pl.multiple_of(i * chunk, chunk), chunk)
        for kind in range(3):
            x = slabs_ref[kind, at, :].astype(f32)
            if kind < 2:
                x = x * lax.rsqrt(mm_split(x * x, head_ones, 2) + 1e-06)
            feats[kind, at, :] = x
        for a in range(per_group):
            head = first + a
            decay = -rate_ref[head] * jnp.exp(gates_ref[i, pl.ds(head, 1), :])
            strength = jax.nn.sigmoid(gates_ref[i, pl.ds(heads + head, 1), :] + bias_ref[head])
            gates[a, at, :] = jnp.broadcast_to(decay, (chunk, chunk)).T
            gates[per_group + a, at, :] = jnp.broadcast_to(strength, (chunk, chunk)).T
        return carry

    lax.fori_loop(0, count // chunk, prepare, 0, unroll=count // chunk <= 4)

    columns = chunk // tall
    flane = lax.broadcasted_iota(jnp.int32, (chunk, width), 1) // dk

    def lanes_of(parts):
        out = parts[0][:, :width]
        for a in range(1, per_group):
            out = jnp.where(flane == a, parts[a][:, :width], out)
        return out

    def stacked(x):
        if per_group == 1:
            return x
        return jnp.concatenate(
            [jnp.where(flane == a, x, jnp.zeros_like(x)) for a in range(per_group)], axis=0
        )

    def side_by_side(parts):
        return parts[0] if per_group == 1 else jnp.concatenate(parts, axis=1)

    def load(ref, which, i, by_column):
        if not by_column:
            return ref[which, pl.ds(pl.multiple_of(i * chunk, chunk), chunk), :]
        return jnp.concatenate(
            [ref[which, pl.ds(i * columns + c, tall, stride=wide), :] for c in range(columns)],
            axis=0,
        )

    states[...] = jnp.zeros_like(states)

    def advance(i, carry):
        work = []
        for order in range(2):
            q, k, v = (load(feats, kind, i, order) for kind in range(3))
            cums, betas, systems, scores = [], [], [], []
            for a in range(per_group):
                cum = split_mm(tri, load(gates, a, i, order), 3)
                beta = load(gates, per_group + a, i, order)
                gap = cum - cum.T
                within = jnp.where(inclusive, jnp.exp(jnp.where(inclusive, gap, 0.0)), 0.0)
                k_a = k if per_group == 1 else jnp.where(flane == a, k, 0.0)
                q_a = q if per_group == 1 else jnp.where(flane == a, q, 0.0)
                dots = mm(jnp.concatenate([k_a, q_a], axis=0), k, ((1,), (1,)))
                systems.append(within * dots[:chunk] * beta)
                scores.append(within * dots[chunk:])
                cums.append(cum)
                betas.append(beta)
            work.append((q, k, v, cums, betas, systems, scores))

        inverses = [[None] * per_group for _ in range(2)]
        half = 1
        while half < chunk:
            here = ((ti // (2 * half)) == (tj // (2 * half))) & (
                (lax.rem(ti, 2 * half) >= half) & (lax.rem(tj, 2 * half) < half)
            )
            lows = [
                [jnp.where(here, work[o][5][a], 0.0) for a in range(per_group)] for o in range(2)
            ]
            if half == 1:
                inverses = [[eye - low for low in row] for row in lows]
            else:
                firsts = [
                    [mm(lows[o][a], inverses[o][a]) for a in range(per_group)] for o in range(2)
                ]
                inverses = [
                    [inverses[o][a] - mm(inverses[o][a], firsts[o][a]) for a in range(per_group)]
                    for o in range(2)
                ]
            half *= 2

        for order in range(2):
            q, k, v, cums, betas, _, scores = work[order]
            beta = lanes_of(betas)
            cum = lanes_of(cums)
            scale = jnp.exp(cum)
            last = cum[chunk - 1 : chunk, :]
            tail = jnp.exp(last - cum)
            both = side_by_side(inverses[order])
            u = mm(both, stacked(v * beta))
            w = mm(both, stacked(k * (beta * scale)))
            state = states[order]
            fresh = u - mm(w, state)
            out = mm(q * scale, state) + mm(side_by_side(scores), stacked(fresh))
            grown = mm(k * tail, fresh, ((0,), (0,)))
            decayed = state * jnp.exp(last)
            states[order] = decayed + jnp.where(same_head, grown, 0.0)
            normed = out * lax.rsqrt(mm_split(out * out, head_ones, 2) * (1.0 / dk) + 1e-06)
            if order == 0:
                row_buf[pl.ds(pl.multiple_of(i * chunk, chunk), chunk), :] = normed
            else:
                normed = normed.astype(bf16).astype(f32)
                for c in range(columns):
                    col_buf[pl.ds(i * columns + c, tall, stride=wide), :] = normed[
                        c * tall : (c + 1) * tall
                    ]
        return carry

    lax.fori_loop(0, count // chunk, advance, 0)

    def finish(s, carry):
        at = pl.ds(s * block, block)
        out_ref[s] = (row_buf[at, :] + col_buf[at, :]).astype(bf16)
        return carry

    lax.fori_loop(0, strips, finish, 0)


def return_kernel(strips, groups, mixed_ref, out_ref, send_sem, recv_sem):
    me_f, me_s = lax.axis_index("face"), lax.axis_index("strip")
    rep = strips // groups
    barrier = pltpu.get_barrier_semaphore()
    for step in range(1, strips):
        pl.semaphore_signal(
            barrier, inc=1, device_id=(me_f, lax.rem(me_s + step, strips)), device_id_type=MESH
        )
    pl.semaphore_wait(barrier, strips - 1)
    mine = group_of(me_s, strips, groups)
    sends = lax.rem(me_s, rep) == 0

    def copy(step):
        dest = lax.rem(me_s + step, strips)
        return pltpu.make_async_remote_copy(
            src_ref=mixed_ref.at[dest],
            dst_ref=out_ref.at[mine],
            send_sem=send_sem.at[step],
            recv_sem=recv_sem.at[mine],
            device_id=(me_f, dest),
            device_id_type=MESH,
        )

    @pl.when(sends)
    def _():
        for step in range(1, strips):
            copy(step).start()
        pltpu.make_async_copy(mixed_ref.at[me_s], out_ref.at[mine], recv_sem.at[mine]).start()
        for step in range(1, strips):
            copy(step).wait_send()

    for group in range(groups):
        pltpu.make_async_copy(mixed_ref.at[0], out_ref.at[group], recv_sem.at[group]).wait()


def scan_call(
    first, slabs, gates, decay_rate, beta_bias, strips, per_group, tall, wide, dk
):
    count, width = slabs.shape[1:]
    block = count // strips
    chunk = min(128, count)
    vmem = pl.BlockSpec(memory_space=pltpu.VMEM)
    smem = pl.BlockSpec(memory_space=pltpu.SMEM)
    return pl.pallas_call(
        functools.partial(scan_kernel, (chunk, per_group, tall, wide, dk)),
        out_shape=jax.ShapeDtypeStruct((strips, block, width), bf16),
        in_specs=[smem, vmem, vmem, smem, smem],
        out_specs=vmem,
        scratch_shapes=[
            pltpu.VMEM((3, count, width), f32),
            pltpu.VMEM((2 * per_group, count, chunk), f32),
            pltpu.VMEM((count, width), f32),
            pltpu.VMEM((count, width), f32),
            pltpu.VMEM((2, width, width), f32),
        ],
        name="scans",
    )(first, slabs, gates, decay_rate, beta_bias)


def on_device(faces, strips, pixels_in, w_qkv, w_gate, decay_rate, beta_bias):
    _, rows_here, wide, features = pixels_in.shape
    heads = decay_rate.shape[0]
    block = rows_here * wide
    count = block * strips
    tall = rows_here * strips
    model = w_qkv.shape[1] * faces // 3
    dk = model // heads
    groups = min(strips, heads)
    per_group = heads // groups
    width = per_group * dk
    n_slab = w_qkv.shape[1] // width
    gate_cols = w_gate.shape[1]
    pieces = 4
    chunk = min(128, count)
    chips = strips // 2
    vmem = pl.BlockSpec(memory_space=pltpu.VMEM)
    dma = pltpu.SemaphoreType.DMA
    if width % 128:
        w_qkv = w_qkv.reshape(features, n_slab, width).transpose(1, 0, 2)
    slabs, gates = pl.pallas_call(
        functools.partial(project_kernel, (faces, strips, groups, n_slab, pieces)),
        out_shape=(
            jax.ShapeDtypeStruct((3, count, width), bf16),
            jax.ShapeDtypeStruct((count // chunk, 2 * heads, chunk), f32),
        ),
        in_specs=[vmem, pl.BlockSpec(memory_space=pl.ANY), vmem],
        out_specs=(vmem, vmem),
        scratch_shapes=[
            pltpu.VMEM((count, features), bf16),
            pltpu.VMEM((3, features, width), bf16),
            pltpu.VMEM((gate_cols, features), f32),
            pltpu.VMEM((faces, gate_cols, features), f32),
            pltpu.VMEM((count, 3 * width), f32),
            dma((chips,)),
            dma((chips,)),
            dma((strips,)),
            dma((3, pieces, 2)),
            dma((3, pieces)),
            dma((faces,)),
            dma((faces,)),
        ],
        compiler_params=pltpu.CompilerParams(collective_id=0, has_side_effects=True),
        name="project",
    )(pixels_in.reshape(block, features), w_qkv, w_gate.T)
    group = group_of(lax.axis_index("strip"), strips, groups)
    first = (group * per_group).astype(jnp.int32).reshape(1)
    mixed = scan_call(
        first, slabs, gates, decay_rate, beta_bias, strips, per_group, tall, wide, dk
    )
    returned = pl.pallas_call(
        functools.partial(return_kernel, strips, groups),
        out_shape=jax.ShapeDtypeStruct((groups, block, width), bf16),
        in_specs=[vmem],
        out_specs=vmem,
        scratch_shapes=[dma((strips,)), dma((groups,))],
        compiler_params=pltpu.CompilerParams(collective_id=1, has_side_effects=True),
        name="give_back",
    )(mixed)
    return returned.transpose(1, 0, 2).reshape(1, rows_here, wide, model)


def solution(mesh):
    in_specs = (P("face", "strip", None, None), P(None, "face"), P(None, "face"), P(), P())
    out_specs = P("face", "strip", None, None)
    return jax.shard_map(
        functools.partial(on_device, mesh.shape["face"], mesh.shape["strip"]),
        mesh=mesh,
        in_specs=in_specs,
        out_specs=out_specs,
        check_vma=False,
    )
```

time: 55.7 us -> 66 us (1.18); the launches traced: 54.7 us -> 65.8 us
  Pallas kernels: 51.4 us -> 64 us
  local copies, waits for them, and re-layouts: 3.28 us -> 1.71 us
    pallas_call x1, Pallas kernels: 6.47 us -> 24.9 us  [on_device(): pl.pallas_call(functools.partial(return_kernel, strips, groups), out_shap...]
    pallas_call x1, Pallas kernels: 30.1 us -> 24.6 us  [on_device(): pl.pallas_call(functools.partial(project_kernel, (faces, strips, groups,...]
    unnamed x1 -> x0, local copies, waits for them, and re-layouts: 1.57 us -> none
where the time goes in v2:
time: 66 us; the launch traced here: 65.8 us
  Pallas kernels  64 us (97%)
  local copies, waits for them, and re-layouts  1.71 us (3%)
    pallas_call x1, Pallas kernels, on_device(): pl.pallas_call(functools.partial(return_kernel, strips, groups), out_shap...  24.9 us
    pallas_call x1, Pallas kernels, on_device(): pl.pallas_call(functools.partial(project_kernel, (faces, strips, groups,...  24.6 us
    pallas_call x1, Pallas kernels, scan_call(): pl.pallas_call(functools.partial(scan_kernel, (chunk, per_group, tall, wi...  14.6 us

profile of v2, /device:TPU:0, one launch (start us, length us, event | category | flops | bytes accessed | tf_op | source)
XLA Modules:
  0.0 65.8 jit_solution(6644265630075066467)
XLA Ops:
  0.0 24.6 %project.1 = (bf16[3,512,128]{2,1,0:T(8,128)(2,1)}, f32[4,32,128]{2,1,0:T(8,128)}) custom-call(bf16[64,1024]{1,0:T(8,128)(2,1)} %bitcast.5, bf16[1024,768]{1,0:T(8,128)(2,1)} %wq_ref.1, bf16[8,1024]{1,0:T(8,128)(2,1)} %bitcast.6), custom_call_target="tpu_custom_call" | custom-call | tf_op jit(solution)/shard_map/project/pallas_call | solution.py:473
  24.6 14.6 %scans.1.mixed_ref = bf16[8,64,128]{2,1,0:T(8,128)(2,1)} custom-call(s32[1]{0:T(128)} %bitcast.first_ref, bf16[3,512,128]{2,1,0:T(8,128)(2,1)} %get-tuple-element.7.slabs_ref, f32[4,32,128]{2,1,0:T(8,128)} %get-tuple-element.8.gates_ref, f32[16]{0:T(128)} %rate_ref.1, f32[16]{0:T(128)} %bias_ref.1), custom_call_target="tpu_custom_call" | custom-call | tf_op jit(solution)/shard_map/scans/pallas_call | solution.py:437
  39.2 24.9 %give_back.1 = bf16[8,64,128]{2,1,0:T(8,128)(2,1)} custom-call(bf16[8,64,128]{2,1,0:T(8,128)(2,1)} %scans.1.mixed_ref), custom_call_target="tpu_custom_call" | custom-call | tf_op jit(solution)/shard_map/give_back/pallas_call | solution.py:503
  64.0 1.0 %copy.6 = bf16[64,8,128]{2,1,0:T(8,128)(2,1)S(1)} copy(bf16[64,8,128]{2,0,1:T(8,128)(2,1)} %bitcast.4) | data formatting | bytes 262144 | tf_op jit(solution)/shard_map/transpose | solution.py:512
  65.0 0.7 %reshape.11 = bf16[1,1,64,1024]{3,2,1,0:T(8,128)(2,1)} reshape(bf16[64,8,128]{2,1,0:T(8,128)(2,1)S(1)} %copy.6) | data formatting | bytes 262144 | tf_op jit(solution)/shard_map/reshape | solution.py:512

commit v3 on v1

--- a/solution.py
+++ b/solution.py
@@ -33,32 +33,55 @@
 
 def project_kernel(
     cfg, px_ref, wq_ref, wg_ref, slabs_ref, gates_ref,
-    px_all, proj, glog, px_send, px_recv, slab_send, slab_recv, gate_send, gate_recv,
+    px_all, proj, glog, weights, weight_sem, px_send, px_recv, slab_send, slab_recv, gate_send, gate_recv,
 ):
     faces, strips, groups, rep, heads, per_group = cfg
     me_f, me_s = lax.axis_index("face"), lax.axis_index("strip")
     n_slab = proj.shape[1]
-    gate_cols = wg_ref.shape[1]
+    gate_cols = wg_ref.shape[0]
     width = proj.shape[3]
     n_gate = gate_cols // per_group
+    block = px_ref.shape[0]
+    half = block // 2
+    fetch = pltpu.make_async_copy(wq_ref, weights, weight_sem)
+    fetch.start()
     greet_all(faces, strips, me_f, me_s)
-
-    def px_copy(step):
-        face = lax.rem(me_f + step, faces)
+    two_sided = jnp.minimum(me_f, faces - 1 - me_f)
+    longer = jnp.where(me_f < faces - 1 - me_f, 1, -1)
+
+    def face_at(step):
+        near = me_f + (step + 1) // 2 * (-1 if step % 2 else 1)
+        return jnp.where(step <= 2 * two_sided, near, me_f + longer * (step - two_sided))
+
+    def px_copy(face, dest, piece, sem, src):
+        rows = pl.ds(piece * half, half)
         return pltpu.make_async_remote_copy(
-            src_ref=px_ref,
-            dst_ref=px_all.at[me_f],
-            send_sem=px_send.at[step],
-            recv_sem=px_recv.at[me_f],
-            device_id=(face, me_s),
+            src_ref=src.at[rows],
+            dst_ref=px_all.at[face, rows],
+            send_sem=sem,
+            recv_sem=px_recv.at[face, piece],
+            device_id=(dest, me_s),
             device_id_type=MESH,
         )
 
-    for step in range(1, faces):
-        px_copy(step).start()
+    def px_out(piece, side):
+        dest = me_f + (1 if side else -1)
+        there = (dest >= 0) & (dest < faces)
+        return there, px_copy(me_f, dest, piece, px_send.at[0, piece, side], px_ref)
+
+    def px_pass(step, piece):
+        face = face_at(step)
+        dest = jnp.where(face < me_f, me_f + 1, me_f - 1)
+        there = (dest >= 0) & (dest < faces)
+        return there, px_copy(face, dest, piece, px_send.at[step, piece, 0], px_all.at[face])
+
+    for piece in range(2):
+        for side in range(2):
+            there, copy = px_out(piece, side)
+            pl.when(there)(copy.start)
 
     def slab_copy(step, j, r):
-        face = lax.rem(me_f + step, faces)
+        face = face_at(step) if step else me_f
         slab = me_f * n_slab + j
         kind, group = slab // groups, lax.rem(slab, groups)
         dest = group * rep + r
@@ -76,7 +99,7 @@
         return remote, local, dest
 
     def gate_copy(step, i, r):
-        face = lax.rem(me_f + step, faces)
+        face = face_at(step) if step else me_f
         first = me_f * gate_cols
         kind, group = first // heads, lax.rem(first, heads) // per_group + i
         dest = group * rep + r
@@ -112,24 +135,38 @@
         if step == 0:
             px = px_ref[...]
         else:
-            face = lax.rem(me_f + step, faces)
-            pltpu.make_async_copy(px_ref, px_all.at[face], px_recv.at[face]).wait()
+            face = face_at(step) if step else me_f
+            for piece in range(2):
+                rows = pl.ds(piece * half, half)
+                pltpu.make_async_copy(
+                    px_ref.at[rows], px_all.at[face, rows], px_recv.at[face, piece]
+                ).wait()
+                there, copy = px_pass(step, piece)
+                pl.when(there)(copy.start)
             px = px_all[face]
-        logits = jnp.dot(px, wg_ref[...], preferred_element_type=f32)
-        glog[step] = logits.astype(bf16).astype(f32).T
+        logits = lax.dot_general(
+            wg_ref[...], px, (((1,), (1,)), ((), ())), preferred_element_type=f32
+        )
+        glog[step] = logits.astype(bf16).astype(f32)
         for i in range(n_gate):
             for r in range(rep):
                 launch(gate_copy(step, i, r), step)
+        if step == 0:
+            fetch.wait()
+        whole = jnp.dot(px, weights[...], preferred_element_type=f32).astype(bf16)
         for j in range(n_slab):
-            proj[step, j] = jnp.dot(
-                px, wq_ref[:, j * width : (j + 1) * width], preferred_element_type=f32
-            ).astype(bf16)
+            proj[step, j] = whole[:, j * width : (j + 1) * width]
         for j in range(n_slab):
             for r in range(rep):
                 launch(slab_copy(step, j, r), step)
 
-    for step in range(1, faces):
-        px_copy(step).wait_send()
+    for piece in range(2):
+        for side in range(2):
+            there, copy = px_out(piece, side)
+            pl.when(there)(copy.wait_send)
+        for step in range(1, faces):
+            there, copy = px_pass(step, piece)
+            pl.when(there)(copy.wait_send)
     for step in range(faces):
         for i in range(n_gate):
             for r in range(rep):
@@ -320,7 +357,7 @@
     lax.fori_loop(0, strips, finish, 0)
 
 
-def return_kernel(faces, strips, mixed_ref, out_ref, send_sem, recv_sem):
+def return_kernel(rep, strips, mixed_ref, out_ref, send_sem, recv_sem):
     me_f, me_s = lax.axis_index("face"), lax.axis_index("strip")
     barrier = pltpu.get_barrier_semaphore()
     for step in range(1, strips):
@@ -329,27 +366,35 @@
         )
     pl.semaphore_wait(barrier, strips - 1)
 
+    width = mixed_ref.shape[2]
+    mine = me_s // rep
+
+    def place(group):
+        if len(out_ref.shape) == 3:
+            return out_ref.at[group]
+        return out_ref.at[:, pl.ds(pl.multiple_of(group * width, width), width)]
+
     def copy(step):
         dest = lax.rem(me_s + step, strips)
         return pltpu.make_async_remote_copy(
             src_ref=mixed_ref.at[dest],
-            dst_ref=out_ref.at[me_s],
+            dst_ref=place(mine),
             send_sem=send_sem.at[step],
-            recv_sem=recv_sem.at[me_s],
+            recv_sem=recv_sem.at[mine],
             device_id=(me_f, dest),
             device_id_type=MESH,
         )
 
-    for step in range(1, strips):
-        copy(step).start()
-    own = pltpu.make_async_copy(mixed_ref.at[me_s], out_ref.at[me_s], recv_sem.at[me_s])
-    own.start()
-    for step in range(1, strips):
-        copy(step).wait_send()
-    for source in range(strips):
-        pltpu.make_async_copy(
-            mixed_ref.at[0], out_ref.at[source], recv_sem.at[source]
-        ).wait()
+    @pl.when(lax.rem(me_s, rep) == 0)
+    def _():
+        for step in range(1, strips):
+            copy(step).start()
+        pltpu.make_async_copy(mixed_ref.at[me_s], place(mine), recv_sem.at[mine]).start()
+        for step in range(1, strips):
+            copy(step).wait_send()
+
+    for group in range(strips // rep):
+        pltpu.make_async_copy(mixed_ref.at[0], place(group), recv_sem.at[group]).wait()
 
 
 def scan_call(first, slabs, gates, decay_rate, beta_bias, per_group, tall, wide, dk):
@@ -396,14 +441,16 @@
             jax.ShapeDtypeStruct((3, strips, block, width), bf16),
             jax.ShapeDtypeStruct((2, strips, gate_cols, block), f32),
         ),
-        in_specs=[vmem, vmem, vmem],
+        in_specs=[vmem, pl.BlockSpec(memory_space=pl.ANY), vmem],
         out_specs=(vmem, vmem),
         scratch_shapes=[
             pltpu.VMEM((faces, block, features), bf16),
             pltpu.VMEM((faces, n_slab, block, width), bf16),
             pltpu.VMEM((faces, gate_cols, block), f32),
-            dma((faces,)),
-            dma((faces,)),
+            pltpu.VMEM(w_qkv.shape, bf16),
+            dma(()),
+            dma((faces, 2, 2)),
+            dma((faces, 2)),
             dma((faces, n_slab, rep)),
             dma((3, strips)),
             dma((faces, n_gate, rep)),
@@ -411,20 +458,24 @@
         ],
         compiler_params=pltpu.CompilerParams(collective_id=0, has_side_effects=True),
         name="project",
-    )(pixels_in.reshape(block, features), w_qkv, w_gate)
+    )(pixels_in.reshape(block, features), w_qkv, w_gate.T)
     first = (lax.axis_index("strip") // rep * per_group).astype(jnp.int32).reshape(1)
     mixed = scan_call(first, slabs, gates, decay_rate, beta_bias, per_group, tall, wide, dk)
+    flat = width % 128 == 0
     returned = pl.pallas_call(
-        functools.partial(return_kernel, faces, strips),
-        out_shape=jax.ShapeDtypeStruct((strips, block, width), bf16),
+        functools.partial(return_kernel, rep, strips),
+        out_shape=jax.ShapeDtypeStruct(
+            (block, model) if flat else (groups, block, width), bf16
+        ),
         in_specs=[vmem],
         out_specs=vmem,
-        scratch_shapes=[dma((strips,)), dma((strips,))],
+        scratch_shapes=[dma((strips,)), dma((groups,))],
         compiler_params=pltpu.CompilerParams(collective_id=1, has_side_effects=True),
         name="give_back",
     )(mixed)
-    whole = returned[::rep].transpose(1, 0, 2)
-    return whole.reshape(1, rows_here, wide, model)
+    if not flat:
+        returned = returned.transpose(1, 0, 2)
+    return returned.reshape(1, rows_here, wide, model)
 
 
 def solution(mesh):

time: 55.7 us -> 56.1 us (level); the launches traced: 54.7 us -> 55.9 us
  Pallas kernels: 51.4 us -> 54.3 us
  local copies, waits for them, and re-layouts: 3.28 us -> 1.57 us
    pallas_call x1, Pallas kernels: 30.1 us -> 33 us  [on_device(): pl.pallas_call(functools.partial(project_kernel, (faces, strips, groups,...]
    transpose x1 -> x0, local copies, waits for them, and re-layouts: 0.99 us -> none  [on_device(): whole = returned[::rep].transpose(1, 0, 2)]
    reshape x1 -> x0, local copies, waits for them, and re-layouts: 0.71 us -> none  [on_device(): return whole.reshape(1, rows_here, wide, model)]
where the time goes in v3:
time: 56.1 us; the launch traced here: 55.9 us
  Pallas kernels  54.3 us (97%)
  local copies, waits for them, and re-layouts  1.57 us (3%)
    pallas_call x1, Pallas kernels, on_device(): pl.pallas_call(functools.partial(project_kernel, (faces, strips, groups,...  33 us
    pallas_call x1, Pallas kernels, scan_call(): pl.pallas_call(functools.partial(scan_kernel, (chunk, per_group, tall, wi...  14.8 us
    pallas_call x1, Pallas kernels, on_device(): pl.pallas_call(functools.partial(return_kernel, rep, strips), out_shape=j...  6.46 us
    unnamed x1, local copies, waits for them, and re-layouts  1.57 us

profile of v3, /device:TPU:0, one launch (start us, length us, event | category | flops | bytes accessed | tf_op | source)
XLA Modules:
  0.0 55.9 jit_solution(567090780180293211)
XLA Ops:
  0.0 33.0 %project.1 = (bf16[3,8,64,128]{3,2,1,0:T(8,128)(2,1)}, f32[2,8,8,64]{3,2,1,0:T(8,128)}) custom-call(bf16[64,1024]{1,0:T(8,128)(2,1)} %bitcast.5, bf16[1024,768]{1,0:T(8,128)(2,1)} %wq_ref.1, bf16[8,1024]{1,0:T(8,128)(2,1)} %bitcast.6), custom_call_target="tpu_custom_call" | custom-call | tf_op jit(solution)/shard_map/project/pallas_call | solution.py:438
  33.0 14.8 %scans.1.mixed_ref = bf16[8,64,128]{2,1,0:T(8,128)(2,1)} custom-call(s32[1]{0:T(128)} %bitcast.first_ref, bf16[3,8,64,128]{3,2,1,0:T(8,128)(2,1)} %get-tuple-element.7.slabs_ref, f32[2,8,8,64]{3,2,1,0:T(8,128)} %get-tuple-element.8.gates_ref, f32[16]{0:T(128)} %rate_ref.1, f32[16]{0:T(128)} %bias_ref.1), custom_call_target="tpu_custom_call" | custom-call | tf_op jit(solution)/shard_map/scans/pallas_call | solution.py:406
  47.8 6.5 %give_back.1 = bf16[64,1024]{1,0:T(8,128)(2,1)} custom-call(bf16[8,64,128]{2,1,0:T(8,128)(2,1)} %scans.1.mixed_ref), custom_call_target="tpu_custom_call" | custom-call | tf_op jit(solution)/shard_map/give_back/pallas_call | solution.py:465
  54.3 1.6 %copy.7 = bf16[1,1,64,1024]{3,2,1,0:T(8,128)(2,1)} copy(bf16[1,1,64,1024]{3,2,1,0:T(8,128)(2,1)} %bitcast.4) | data formatting | bytes 262144

commit v4 on v3

--- a/solution.py
+++ b/solution.py
@@ -131,34 +131,41 @@
         else:
             remote.wait_send()
 
-    for step in range(faces):
-        if step == 0:
-            px = px_ref[...]
-        else:
-            face = face_at(step) if step else me_f
-            for piece in range(2):
-                rows = pl.ds(piece * half, half)
-                pltpu.make_async_copy(
-                    px_ref.at[rows], px_all.at[face, rows], px_recv.at[face, piece]
-                ).wait()
-                there, copy = px_pass(step, piece)
-                pl.when(there)(copy.start)
-            px = px_all[face]
+    def work_on(step, px):
         logits = lax.dot_general(
             wg_ref[...], px, (((1,), (1,)), ((), ())), preferred_element_type=f32
         )
         glog[step] = logits.astype(bf16).astype(f32)
+        whole = jnp.dot(px, weights[...], preferred_element_type=f32).astype(bf16)
+        for j in range(n_slab):
+            proj[step, j] = whole[:, j * width : (j + 1) * width]
+
+    def send_out(step):
         for i in range(n_gate):
             for r in range(rep):
                 launch(gate_copy(step, i, r), step)
-        if step == 0:
-            fetch.wait()
-        whole = jnp.dot(px, weights[...], preferred_element_type=f32).astype(bf16)
-        for j in range(n_slab):
-            proj[step, j] = whole[:, j * width : (j + 1) * width]
         for j in range(n_slab):
             for r in range(rep):
                 launch(slab_copy(step, j, r), step)
+
+    fetch.wait()
+    work_on(0, px_ref[...])
+    send_out(0)
+    for step in range(1, faces):
+        face = face_at(step)
+        for piece in range(2):
+            rows = pl.ds(piece * half, half)
+            pltpu.make_async_copy(
+                px_ref.at[rows], px_all.at[face, rows], px_recv.at[face, piece]
+            ).wait()
+            there, copy = px_pass(step, piece)
+            pl.when(there)(copy.start)
+        if step < faces - 1:
+            work_on(step, px_all[face])
+    for step in range(1, faces - 1):
+        send_out(step)
+    work_on(faces - 1, px_all[face_at(faces - 1)])
+    send_out(faces - 1)
 
     for piece in range(2):
         for side in range(2):
@@ -280,62 +287,67 @@
 
     states[...] = jnp.zeros_like(states)
 
-    def advance(i, carry):
-        work = []
-        for order in range(2):
-            q, k, v = (load(feats, kind, i, order) for kind in range(3))
-            cums, betas, systems, scores = [], [], [], []
-            for a in range(per_group):
-                cum = split_mm(tri, load(gates, a, i, order), 3)
-                beta = load(gates, per_group + a, i, order)
-                gap = cum - cum.T
-                within = jnp.where(inclusive, jnp.exp(jnp.where(inclusive, gap, 0.0)), 0.0)
-                k_a = k if per_group == 1 else jnp.where(flane == a, k, 0.0)
-                q_a = q if per_group == 1 else jnp.where(flane == a, q, 0.0)
-                dots = mm(jnp.concatenate([k_a, q_a], axis=0), k, ((1,), (1,)))
-                systems.append(within * dots[:chunk] * beta)
-                scores.append(within * dots[chunk:])
-                cums.append(cum)
-                betas.append(beta)
-            work.append((q, k, v, cums, betas, systems, scores))
-
-        inverses = [[None] * per_group for _ in range(2)]
+    per_turn = 2 if (count // chunk) % 2 == 0 else 1
+    units = [(m, order, a) for m in range(per_turn) for order in range(2) for a in range(per_group)]
+
+    def advance(turn, carry):
+        base = turn * per_turn
+        inputs, cums, betas, systems, scores = {}, {}, {}, {}, {}
+        for m in range(per_turn):
+            for order in range(2):
+                inputs[m, order] = [load(feats, kind, base + m, order) for kind in range(3)]
+        for unit in units:
+            m, order, a = unit
+            q, k, _ = inputs[m, order]
+            cum = split_mm(tri, load(gates, a, base + m, order), 3)
+            beta = load(gates, per_group + a, base + m, order)
+            gap = cum - cum.T
+            within = jnp.where(inclusive, jnp.exp(jnp.where(inclusive, gap, 0.0)), 0.0)
+            k_a = k if per_group == 1 else jnp.where(flane == a, k, 0.0)
+            q_a = q if per_group == 1 else jnp.where(flane == a, q, 0.0)
+            dots = mm(jnp.concatenate([k_a, q_a], axis=0), k, ((1,), (1,)))
+            systems[unit] = within * dots[:chunk] * beta
+            scores[unit] = (within * dots[chunk:]).astype(bf16)
+            cums[unit] = cum
+            betas[unit] = beta
+
+        inverses = {}
         half = 1
         while half < chunk:
             here = ((ti // (2 * half)) == (tj // (2 * half))) & (
                 (lax.rem(ti, 2 * half) >= half) & (lax.rem(tj, 2 * half) < half)
             )
-            lows = [
-                [jnp.where(here, work[o][5][a], 0.0) for a in range(per_group)] for o in range(2)
-            ]
+            lows = {u: jnp.where(here, systems[u], 0.0) for u in units}
             if half == 1:
-                inverses = [[eye - low for low in row] for row in lows]
+                inverses = {u: eye - lows[u] for u in units}
             else:
-                firsts = [
-                    [mm(lows[o][a], inverses[o][a]) for a in range(per_group)] for o in range(2)
-                ]
-                inverses = [
-                    [inverses[o][a] - mm(inverses[o][a], firsts[o][a]) for a in range(per_group)]
-                    for o in range(2)
-                ]
+                firsts = {u: mm(lows[u], inverses[u]) for u in units}
+                inverses = {u: inverses[u] - mm(inverses[u], firsts[u]) for u in units}
             half *= 2
 
-        for order in range(2):
-            q, k, v, cums, betas, _, scores = work[order]
-            beta = lanes_of(betas)
-            cum = lanes_of(cums)
+        pairs = [(m, order) for m in range(per_turn) for order in range(2)]
+        ready = {}
+        for m, order in pairs:
+            q, k, v = inputs[m, order]
+            mine = [(m, order, a) for a in range(per_group)]
+            beta = lanes_of([betas[u] for u in mine])
+            cum = lanes_of([cums[u] for u in mine])
             scale = jnp.exp(cum)
             last = cum[chunk - 1 : chunk, :]
-            tail = jnp.exp(last - cum)
-            both = side_by_side(inverses[order])
-            u = mm(both, stacked(v * beta))
-            w = mm(both, stacked(k * (beta * scale)))
+            both = side_by_side([inverses[u].astype(bf16) for u in mine])
+            u_part = mm(both, stacked((v * beta).astype(bf16)))
+            w_part = mm(both, stacked((k * (beta * scale)).astype(bf16)))
+            keys_out = (k * jnp.exp(last - cum)).astype(bf16)
+            reads = side_by_side([scores[u] for u in mine])
+            ready[m, order] = (u_part, w_part, q * scale, keys_out, reads, jnp.exp(last))
+        for m, order in pairs:
+            u_part, w_part, q_part, keys_out, reads, end = ready[m, order]
+            i = base + m
             state = states[order]
-            fresh = u - mm(w, state)
-            out = mm(q * scale, state) + mm(side_by_side(scores), stacked(fresh))
-            grown = mm(k * tail, fresh, ((0,), (0,)))
-            decayed = state * jnp.exp(last)
-            states[order] = decayed + jnp.where(same_head, grown, 0.0)
+            fresh = u_part - mm(w_part, state)
+            out = mm(q_part, state) + mm(reads, stacked(fresh.astype(bf16)))
+            grown = mm(keys_out, fresh, ((0,), (0,)))
+            states[order] = state * end + jnp.where(same_head, grown, 0.0)
             normed = out * lax.rsqrt(mm_split(out * out, head_ones, 2) * (1.0 / dk) + 1e-06)
             if order == 0:
                 row_buf[pl.ds(pl.multiple_of(i * chunk, chunk), chunk), :] = normed
@@ -347,7 +359,7 @@
                     ]
         return carry
 
-    lax.fori_loop(0, count // chunk, advance, 0)
+    lax.fori_loop(0, count // chunk // per_turn, advance, 0)
 
     def finish(s, carry):
         at = pl.ds(s * block, block)

time: 56.1 us -> 49.5 us (0.88)
  Pallas kernels: 54.3 us -> 47.7 us
    pallas_call x1, Pallas kernels: 14.8 us -> 9.64 us  [scan_call(): pl.pallas_call(functools.partial(scan_kernel, (chunk, per_group, tall, wi...]
    pallas_call x1, Pallas kernels: 33 us -> 31.6 us  [on_device(): pl.pallas_call(functools.partial(project_kernel, (faces, strips, groups,...]
where the time goes in v4:
time: 49.5 us; the launch traced here: 49.3 us
  Pallas kernels  47.7 us (96%)
  local copies, waits for them, and re-layouts  1.57 us (3%)
    pallas_call x1, Pallas kernels, on_device(): pl.pallas_call(functools.partial(project_kernel, (faces, strips, groups,...  31.6 us
    pallas_call x1, Pallas kernels, scan_call(): pl.pallas_call(functools.partial(scan_kernel, (chunk, per_group, tall, wi...  9.64 us
    pallas_call x1, Pallas kernels, on_device(): pl.pallas_call(functools.partial(return_kernel, rep, strips), out_shape=j...  6.46 us
    unnamed x1, local copies, waits for them, and re-layouts  1.57 us

profile of v4, /device:TPU:0, one launch (start us, length us, event | category | flops | bytes accessed | tf_op | source)
XLA Modules:
  0.0 49.3 jit_solution(12052548386817889955)
XLA Ops:
  0.0 31.6 %project.1 = (bf16[3,8,64,128]{3,2,1,0:T(8,128)(2,1)}, f32[2,8,8,64]{3,2,1,0:T(8,128)}) custom-call(bf16[64,1024]{1,0:T(8,128)(2,1)} %bitcast.5, bf16[1024,768]{1,0:T(8,128)(2,1)} %wq_ref.1, bf16[8,1024]{1,0:T(8,128)(2,1)} %bitcast.6), custom_call_target="tpu_custom_call" | custom-call | tf_op jit(solution)/shard_map/project/pallas_call | solution.py:450
  31.6 9.6 %scans.1.mixed_ref = bf16[8,64,128]{2,1,0:T(8,128)(2,1)} custom-call(s32[1]{0:T(128)} %bitcast.first_ref, bf16[3,8,64,128]{3,2,1,0:T(8,128)(2,1)} %get-tuple-element.7.slabs_ref, f32[2,8,8,64]{3,2,1,0:T(8,128)} %get-tuple-element.8.gates_ref, f32[16]{0:T(128)} %rate_ref.1, f32[16]{0:T(128)} %bias_ref.1), custom_call_target="tpu_custom_call" | custom-call | tf_op jit(solution)/shard_map/scans/pallas_call | solution.py:418
  41.3 6.5 %give_back.1 = bf16[64,1024]{1,0:T(8,128)(2,1)} custom-call(bf16[8,64,128]{2,1,0:T(8,128)(2,1)} %scans.1.mixed_ref), custom_call_target="tpu_custom_call" | custom-call | tf_op jit(solution)/shard_map/give_back/pallas_call | solution.py:477
  47.7 1.6 %copy.7 = bf16[1,1,64,1024]{3,2,1,0:T(8,128)(2,1)} copy(bf16[1,1,64,1024]{3,2,1,0:T(8,128)(2,1)} %bitcast.4) | data formatting | bytes 262144

commit v5 on v4

--- a/solution.py
+++ b/solution.py
@@ -287,7 +287,7 @@
 
     states[...] = jnp.zeros_like(states)
 
-    per_turn = 2 if (count // chunk) % 2 == 0 else 1
+    per_turn = 4 if count // chunk == 4 else (2 if (count // chunk) % 2 == 0 else 1)
     units = [(m, order, a) for m in range(per_turn) for order in range(2) for a in range(per_group)]
 
     def advance(turn, carry):

time: 49.5 us -> 47.5 us (0.960)
  Pallas kernels: 47.7 us -> 45.7 us
    pallas_call x1, Pallas kernels: 9.64 us -> 7.63 us  [scan_call(): pl.pallas_call(functools.partial(scan_kernel, (chunk, per_group, tall, wi...]
where the time goes in v5:
time: 47.5 us; the launch traced here: 47.3 us
  Pallas kernels  45.7 us (96%)
  local copies, waits for them, and re-layouts  1.57 us (3%)
    pallas_call x1, Pallas kernels, on_device(): pl.pallas_call(functools.partial(project_kernel, (faces, strips, groups,...  31.6 us
    pallas_call x1, Pallas kernels, scan_call(): pl.pallas_call(functools.partial(scan_kernel, (chunk, per_group, tall, wi...  7.63 us
    pallas_call x1, Pallas kernels, on_device(): pl.pallas_call(functools.partial(return_kernel, rep, strips), out_shape=j...  6.46 us
    unnamed x1, local copies, waits for them, and re-layouts  1.57 us

profile of v5, /device:TPU:0, one launch (start us, length us, event | category | flops | bytes accessed | tf_op | source)
XLA Modules:
  0.0 47.3 jit_solution(14952339940569450787)
XLA Ops:
  0.0 31.6 %project.1 = (bf16[3,8,64,128]{3,2,1,0:T(8,128)(2,1)}, f32[2,8,8,64]{3,2,1,0:T(8,128)}) custom-call(bf16[64,1024]{1,0:T(8,128)(2,1)} %bitcast.5, bf16[1024,768]{1,0:T(8,128)(2,1)} %wq_ref.1, bf16[8,1024]{1,0:T(8,128)(2,1)} %bitcast.6), custom_call_target="tpu_custom_call" | custom-call | tf_op jit(solution)/shard_map/project/pallas_call | solution.py:450
  31.6 7.6 %scans.1.mixed_ref = bf16[8,64,128]{2,1,0:T(8,128)(2,1)} custom-call(s32[1]{0:T(128)} %bitcast.first_ref, bf16[3,8,64,128]{3,2,1,0:T(8,128)(2,1)} %get-tuple-element.7.slabs_ref, f32[2,8,8,64]{3,2,1,0:T(8,128)} %get-tuple-element.8.gates_ref, f32[16]{0:T(128)} %rate_ref.1, f32[16]{0:T(128)} %bias_ref.1), custom_call_target="tpu_custom_call" | custom-call | tf_op jit(solution)/shard_map/scans/pallas_call | solution.py:418
  39.2 6.5 %give_back.1 = bf16[64,1024]{1,0:T(8,128)(2,1)} custom-call(bf16[8,64,128]{2,1,0:T(8,128)(2,1)} %scans.1.mixed_ref), custom_call_target="tpu_custom_call" | custom-call | tf_op jit(solution)/shard_map/give_back/pallas_call | solution.py:477
  45.7 1.6 %copy.7 = bf16[1,1,64,1024]{3,2,1,0:T(8,128)(2,1)} copy(bf16[1,1,64,1024]{3,2,1,0:T(8,128)(2,1)} %bitcast.4) | data formatting | bytes 262144
